TPU v7x, 512 devices: a whole 4x8x8 slice. The times are simulated.
512 devices in a mesh: seq: 64 (over y, x, core), head: 8 (over z).
Axes of the slice: x: 4, y: 8, z: 8, core: 2. Of those that a mesh axis runs over, the one named last changes fastest.
Arguments:
- hidden_states: bfloat16 [49152, 8192], P('seq', 'head'), may hold values from -6 to 6
- k_weight: bfloat16 [8192, 1024], P('head', 'seq'), may hold values from -0.0625 to 0.0625
- v_weight: bfloat16 [8192, 1024], P('head', 'seq'), may hold values from -0.0625 to 0.0625
- assignments: int32 [8, 49152], P('head', 'seq'), may hold values from 0 to 1023
- old_centroids: float32 [8, 1024, 128], P('head'), may hold values from -6 to 6
Outputs:
- key_cache: bfloat16 [49152, 1024], P('seq', 'head')
- value_cache: bfloat16 [49152, 1024], P('seq', 'head')
- new_centroids: float32 [8, 1024, 128], P('head', 'seq')
- distances: bfloat16 [8, 49152, 1024], P('head', 'seq')
All inputs are finite; a program needn't handle non-finite values.
Results may differ from a plain program's by a relative error of at most 0.017.
Values may be sent and summed in bfloat16 or wider, within the bound.
A program may use at most 64 MiB of HBM per device.

v0:
```python
import jax
import jax.numpy as jnp
from jax import lax
from jax.sharding import PartitionSpec as P


def shards(hidden_states, k_weight, v_weight, assignments, old_centroids):
    tok_rows = hidden_states.shape[0]
    heads_local = old_centroids.shape[0]
    clusters = old_centroids.shape[1]
    head_size = old_centroids.shape[2]
    stacked = jnp.stack((k_weight, v_weight), axis=1)
    partial_terms = jnp.einsum(
        "td,dkc->tkc",
        hidden_states,
        lax.all_gather(stacked, "seq", axis=2, tiled=True),
        preferred_element_type=jnp.float32,
    )
    summed = lax.psum_scatter(
        partial_terms.astype(jnp.bfloat16), "head", scatter_dimension=2, tiled=True
    ).astype(jnp.float32)
    key_cache = summed[:, 0].astype(jnp.bfloat16)
    value_cache = summed[:, 1].astype(jnp.bfloat16)
    key_heads = key_cache.reshape(tok_rows, heads_local, head_size)
    onehot = (
        assignments[:, :, None] == jnp.arange(clusters, dtype=jnp.int32)[None, None, :]
    ).astype(jnp.bfloat16)
    local_sums = jnp.einsum("htc,the->che", onehot, key_heads, preferred_element_type=jnp.float32)
    local_counts = jnp.swapaxes(jnp.sum(onehot, axis=1, dtype=jnp.float32), 0, 1)
    prior_weight = float(tok_rows * lax.axis_size("seq") // clusters)
    old_turned = jnp.swapaxes(old_centroids, 0, 1)
    share_rows = clusters // lax.axis_size("seq")
    first_row = lax.axis_index("seq") * share_rows
    total_sums, total_counts = lax.psum((local_sums, local_counts), "seq")
    updated = (total_sums + prior_weight * old_turned) / (total_counts[:, :, None] + prior_weight)
    centroid_low = updated.astype(jnp.bfloat16)
    own_rows = lax.dynamic_slice_in_dim(updated, first_row, share_rows, 0)
    new_centroids = jnp.swapaxes(own_rows, 0, 1)
    centroid_wide = centroid_low.astype(jnp.float32)
    centroid_square = jnp.swapaxes(jnp.sum(centroid_wide * centroid_wide, axis=2), 0, 1)
    key_wide = key_heads.astype(jnp.float32)
    key_square = jnp.swapaxes(jnp.sum(key_wide * key_wide, axis=2), 0, 1)
    cross_term = jnp.einsum(
        "the,che->htc", key_heads, centroid_low, preferred_element_type=jnp.float32
    )
    dist = (key_square[:, :, None] - 2.0 * cross_term + centroid_square[:, None, :]) / head_size
    return (key_cache, value_cache, new_centroids, dist.astype(jnp.bfloat16))


def solution(mesh):
    in_specs = (
        P("seq", "head"),
        P("head", "seq"),
        P("head", "seq"),
        P("head", "seq"),
        P("head", None, None),
    )
    out_specs = (P("seq", "head"), P("seq", "head"), P("head", "seq", None), P("head", "seq", None))
    return jax.shard_map(shards, mesh=mesh, in_specs=in_specs, out_specs=out_specs, check_vma=False)
```

profile of v0, /device:TPU:2, one launch (start us, length us, event | category | flops | bytes accessed | tf_op | source)
XLA Modules:
  0.0 438.8 jit_solution(4969922273733050903)
XLA Ops:
  7.2 0.0 all-gather.2.cloned.1.call-start
  7.2 1.5 pad_maximum_fusion
  8.7 0.0 all-gather.2.cloned.1.call-update
  8.8 0.0 reduce-scatter.2.cloned.1.call-start
  8.8 90.7 %all-gather.2.cloned.1.call-done = bf16[1024,2,1024]{0,2,1:T(8,128)(2,1)} async-done(((bf16[1024,2,16]{0,2,1:T(8,128)(2,1)}), bf16[1024,2,1024]{0,2,1:T(8,128)(2,1)}) %all-gather.2.cloned.1.call-update) | async-done | bytes 4194320 | tf_op jit(solution)/shard_map/all_gather | solution.py:16
  99.6 7.4 %convert_bitcast_fusion = bf16[768,2,1024]{0,2,1:T(8,128)(2,1)} fusion(bf16[1024,2,1024]{0,2,1:T(8,128)(2,1)} %all-gather.2.cloned.1.call-done, bf16[768,1024]{1,0:T(8,128)(2,1)S(1)} %copy-done), kind=kOutput, calls=%fused_computation.4 | convolution fusion | flops 3222798336 | bytes 8912896 | tf_op jit(solution)/shard_map/td,dkc->tkc/dot_general | solution.py:13
  106.9 0.0 reduce-scatter.2.cloned.1.call-update
  106.9 0.0 all-reduce.2.cloned.1.call-start
  107.0 1.0 copy-done.2
  108.0 0.2 copy.16
  108.2 0.4 convert_reduce_fusion
  108.6 122.6 %psum.15 = f32[1024,1]{0,1:T(1,128)S(1)} all-reduce(f32[1024,1]{0,1:T(1,128)S(1)} %bitcast.40), channel_id=1, replica_groups=mesh['seq'=64,'head'=8] {'seq'}, use_global_device_ids=true, to_apply=%region_3.0 | all-reduce | flops 1024 | bytes 8192 | tf_op jit(solution)/shard_map/psum | solution.py:34
  231.2 0.0 reduce-scatter.2.cloned.1.call-done
  231.3 2.6 fusion.7
  233.9 0.0 all-reduce.2.cloned.1.call-update
  233.9 1.0 slice_bitcast_fusion
  235.0 0.8 copy.18
  235.8 0.8 copy.19
  236.6 0.1 multiply_reduce_fusion.1
  236.6 191.9 %all-reduce.2.cloned.1.call-done = f32[1024,1,128]{0,2,1:T(8,128)} async-done(((f32[1024,1,128]{0,2,1:T(8,128)}), f32[1024,1,128]{0,2,1:T(8,128)}) %all-reduce.2.cloned.1.call-update) | async-done | bytes 524304 | tf_op jit(solution)/shard_map/psum | solution.py:34
  428.5 1.2 multiply_reduce_fusion
  429.7 0.1 constant_dynamic-slice_fusion
  429.8 0.7 copy.17
  430.4 1.8 fusion.6
  (9 shorter events, 0.0 us)
Async XLA Ops:
  7.2 92.4 %copy-start = (bf16[768,1024]{1,0:T(8,128)(2,1)S(1)}, bf16[768,1024]{1,0:T(8,128)(2,1)}, u32[]{:S(2)}) copy-start(bf16[768,1024]{1,0:T(8,128)(2,1)} %param.5) | copy-start | bytes 4718596
  7.2 92.4 %all-gather.2.cloned.1.call-start = ((), (), s32[]{:S(2)}) async-start(), calls=%async_computation.1 | async-start | bytes 4259840 | tf_op jit(solution)/shard_map/all_gather | solution.py:16
  8.8 222.5 %reduce-scatter.2.cloned.1.call-start = ((), (), s32[]{:S(2)}) async-start(), calls=%async_computation.2 | async-start | bytes 3538944 | tf_op jit(solution)/shard_map/reduce_scatter | solution.py:19
  106.9 1.0 copy-start.2
  106.9 1.2 copy-start.3
  106.9 321.6 %all-reduce.2.cloned.1.call-start = ((), (), s32[]{:S(2)}) async-start(), calls=%async_computation.3 | async-start | bytes 1048576 | tf_op jit(solution)/shard_map/psum | solution.py:34
  231.3 5.3 %copy-start.1 = (bf16[768,2,128]{0,2,1:T(8,128)(2,1)S(1)}, bf16[768,2,128]{0,2,1:T(8,128)(2,1)}, u32[]{:S(2)}) copy-start(bf16[768,2,128]{0,2,1:T(8,128)(2,1)} %reduce-scatter.2.cloned.1.call-done) | copy-start | bytes 1179652
Sparse Core Ops, SparseCore 0:
  12.0 87.5 all-gather.1
  107.1 49.0 reduce-scatter.1
  234.0 194.4 all-reduce.1
where the time goes:
time: 439 us
  waiting for transfers between devices  283 us (64%)
  blocking collectives  123 us (28%)
  between operations  13.8 us (3%)
  matrix products  11.8 us (3%)
  local copies, waits for them, and re-layouts  4.61 us (1%)
    psum x1, waiting for transfers between devices, shards(): total_sums, total_counts = lax.psum((local_sums, local_counts), 'seq')  192 us
    psum x1, blocking collectives, shards(): total_sums, total_counts = lax.psum((local_sums, local_counts), 'seq')  123 us
    all_gather x1, waiting for transfers between devices, shards(): lax.all_gather(stacked, 'seq', axis=2, tiled=True)  90.7 us
  transfers between devices with their start and end apart: 3, of which 2 were waited for; matrix products, arithmetic and copies ran while one was open for 1% of the time, Pallas kernels for 0%

commit v1 on v0

--- a/solution.py
+++ b/solution.py
@@ -2,6 +2,11 @@
 import jax.numpy as jnp
 from jax import lax
 from jax.sharding import PartitionSpec as P
+
+
+def gather_by_exchange(x, axis, dim):
+    copies = jnp.concatenate([x] * lax.axis_size(axis), axis=dim)
+    return lax.all_to_all(copies, axis, dim, dim, tiled=True)
 
 
 def shards(hidden_states, k_weight, v_weight, assignments, old_centroids):
@@ -13,7 +18,7 @@
     partial_terms = jnp.einsum(
         "td,dkc->tkc",
         hidden_states,
-        lax.all_gather(stacked, "seq", axis=2, tiled=True),
+        gather_by_exchange(stacked, "seq", 2),
         preferred_element_type=jnp.float32,
     )
     summed = lax.psum_scatter(

time: 439 us -> 524 us (1.19)
  blocking collectives: 123 us -> 226 us
  waiting for transfers between devices: 283 us -> 194 us
  other arithmetic: 3.13 us -> 67.2 us
  local copies, waits for them, and re-layouts: 4.61 us -> 10.6 us
    all_to_all x0 -> x1, blocking collectives: none -> 107 us  [gather_by_exchange(): return lax.all_to_all(copies, axis, dim, dim, tiled=True)]
    all_gather x1 -> x0, waiting for transfers between devices: 90.7 us -> none  [shards(): lax.all_gather(stacked, 'seq', axis=2, tiled=True)]
    unnamed x1 -> x64, other arithmetic: 0.02 us -> 64.1 us
    concatenate x0 -> x1, local copies, waits for them, and re-layouts: none -> 6.5 us  [gather_by_exchange(): copies = jnp.concatenate([x] * lax.axis_size(axis), axis=dim)]
  transfers between devices with their start and end apart: 3 -> 2, of which waited for: 2 -> 1; matrix products, arithmetic and copies ran while one was open for 1% -> 1% of each run, Pallas kernels for 0% -> 0%
where the time goes in v1:
time: 524 us; the launch traced here: 522 us
  blocking collectives  226 us (43%)
  waiting for transfers between devices  194 us (37%)
  other arithmetic  67.2 us (13%)
  between operations  14.2 us (3%)
  local copies, waits for them, and re-layouts  10.6 us (2%)
  matrix products  9.48 us (2%)
    psum x1, waiting for transfers between devices, shards(): total_sums, total_counts = lax.psum((local_sums, local_counts), 'seq')  194 us
    psum x1, blocking collectives, shards(): total_sums, total_counts = lax.psum((local_sums, local_counts), 'seq')  119 us
    all_to_all x1, blocking collectives, gather_by_exchange(): return lax.all_to_all(copies, axis, dim, dim, tiled=True)  107 us
    unnamed x64, other arithmetic  64.1 us
  transfers between devices with their start and end apart: 2, of which 1 were waited for; matrix products, arithmetic and copies ran while one was open for 1% of the time, Pallas kernels for 0%

profile of v1, /device:TPU:2, one launch (start us, length us, event | category | flops | bytes accessed | tf_op | source)
XLA Modules:
  0.0 521.7 jit_solution(4760827787588277690)
XLA Ops:
  7.2 1.5 constant_dynamic-update-slice_fusion.63
  8.7 1.4 constant_dynamic-update-slice_fusion.62
  11.5 1.4 constant_dynamic-update-slice_fusion.60
  14.3 1.4 constant_dynamic-update-slice_fusion.58
  17.1 1.4 constant_dynamic-update-slice_fusion.56
  21.3 1.4 constant_dynamic-update-slice_fusion.53
  24.1 1.4 constant_dynamic-update-slice_fusion.51
  28.3 1.4 constant_dynamic-update-slice_fusion.48
  31.1 1.4 constant_dynamic-update-slice_fusion.46
  35.3 1.4 constant_dynamic-update-slice_fusion.43
  36.7 1.4 constant_dynamic-update-slice_fusion.42
  38.1 1.4 constant_dynamic-update-slice_fusion.41
  39.5 1.4 constant_dynamic-update-slice_fusion.40
  43.7 1.4 constant_dynamic-update-slice_fusion.37
  45.1 1.4 constant_dynamic-update-slice_fusion.36
  47.9 1.4 constant_dynamic-update-slice_fusion.34
  49.3 1.4 constant_dynamic-update-slice_fusion.33
  72.0 6.5 %copy.27 = bf16[1024,2,1024]{0,1,2:T(2,128)(2,1)S(1)} copy(bf16[1024,2,1024]{0,2,1:T(8,128)(2,1)} %constant_dynamic-update-slice_fusion) | data formatting | bytes 8388608 | tf_op jit(solution)/shard_map/concatenate | solution.py:8
  78.5 106.7 %all_to_all.5 = bf16[1024,2,1024]{0,1,2:T(2,128)(2,1)S(1)} all-to-all(bf16[1024,2,1024]{0,1,2:T(2,128)(2,1)S(1)} %copy.27), channel_id=1, replica_groups=mesh['seq'=64,'head'=8] {'seq'}, dimensions={2} | all-to-all | bytes 8388608 | tf_op jit(solution)/shard_map/all_to_all | solution.py:9
  185.2 5.1 convert_bitcast_fusion
  191.3 119.0 %psum.15 = f32[1024,1]{0,1:T(1,128)S(1)} all-reduce(f32[1024,1]{0,1:T(1,128)S(1)} %bitcast.165), channel_id=1, replica_groups=mesh['seq'=64,'head'=8] {'seq'}, use_global_device_ids=true, to_apply=%region_3.0 | all-reduce | flops 1024 | bytes 8192 | tf_op jit(solution)/shard_map/psum | solution.py:39
  310.4 2.6 fusion.11
  316.7 194.4 %all-reduce.2.cloned.1.call-done = f32[1024,1,128]{0,2,1:T(8,128)} async-done(((f32[1024,1,128]{0,2,1:T(8,128)}), f32[1024,1,128]{0,2,1:T(8,128)}) %all-reduce.2.cloned.1.call-update) | async-done | bytes 524304 | tf_op jit(solution)/shard_map/psum | solution.py:39
  513.0 1.8 fusion.10
  (75 shorter events, 47.5 us)
Async XLA Ops:
  7.2 178.0 %copy-start = (bf16[768,1024]{1,0:T(8,128)(2,1)S(1)}, bf16[768,1024]{1,0:T(8,128)(2,1)}, u32[]{:S(2)}) copy-start(bf16[768,1024]{1,0:T(8,128)(2,1)} %param.5) | copy-start | bytes 4718596
  7.2 44.9 %copy-start.2 = (bf16[1024,16]{0,1:T(8,128)(2,1)S(1)}, bf16[1024,16]{0,1:T(8,128)(2,1)}, u32[]{:S(2)}) copy-start(bf16[1024,16]{0,1:T(8,128)(2,1)} %param.6) | copy-start | bytes 98308
  7.2 44.9 %copy-start.1 = (bf16[1024,16]{0,1:T(8,128)(2,1)S(1)}, bf16[1024,16]{0,1:T(8,128)(2,1)}, u32[]{:S(2)}) copy-start(bf16[1024,16]{0,1:T(8,128)(2,1)} %param.7) | copy-start | bytes 98308
  7.2 303.1 %reduce-scatter.2.cloned.1.call-start = ((), (), s32[]{:S(2)}) async-start(), calls=%async_computation.2 | async-start | bytes 3538944 | tf_op jit(solution)/shard_map/reduce_scatter | solution.py:24
  185.2 5.1 copy-start.4
  190.2 0.7 copy-start.5
  190.2 320.8 %all-reduce.2.cloned.1.call-start = ((), (), s32[]{:S(2)}) async-start(), calls=%async_computation.3 | async-start | bytes 1048576 | tf_op jit(solution)/shard_map/psum | solution.py:39
  310.4 202.7 %copy-start.3 = (bf16[768,2,128]{0,2,1:T(8,128)(2,1)S(1)}, bf16[768,2,128]{0,2,1:T(8,128)(2,1)}, u32[]{:S(2)}) copy-start(bf16[768,2,128]{0,2,1:T(8,128)(2,1)} %reduce-scatter.2.cloned.1.call-done) | copy-start | bytes 1179652
Sparse Core Ops, SparseCore 0:
  190.4 49.4 reduce-scatter.1
  313.1 197.9 all-reduce.1
